TPU v7x, 256 devices: a whole 4x4x8 slice. The times are simulated.
256 devices in a mesh: dp: 8 (over y, z_hi), expert: 32 (over z_lo, x, core).
Axes of the slice: x: 4, y: 4, z: 8 (z_hi: 2, z_lo: 4; z = z_hi * 4 + z_lo), core: 2. Of those that a mesh axis runs over, the one named last changes fastest.
Arguments:
- activations: bfloat16 [32768, 4096], P(('dp', 'expert')), may hold values from -6 to 6
- cotangent: bfloat16 [32768, 4096], P(('dp', 'expert')), may hold values from -6 to 6
- expert_ids: int32 [32768, 1], P(('dp', 'expert')), may hold values from 0 to 127; in each aligned block of 128 rows (0 to 127, 128 to 255, ...) at most 2 rows name the same one
- gate_probs: float32 [32768, 1], P(('dp', 'expert')), may hold values from 0.2 to 1
- gate_up: bfloat16 [32, 2, 4096, 1536], P('expert', None, None, 'dp'), may hold values from -0.09375 to 0.09375
- down_proj: bfloat16 [32, 1536, 4096], P('expert', 'dp'), may hold values from -0.15625 to 0.15625
Outputs:
- input_grad: bfloat16 [32768, 4096], P(('dp', 'expert'))
- grad_gate_up: bfloat16 [32, 2, 4096, 1536], P('expert', None, None, 'dp')
- grad_down: bfloat16 [32, 1536, 4096], P('expert', 'dp')
Inputs may be any that keep to these rules, and one draw needn't show every extreme that they name: `expert_ids`: expert e < 32 is held by index e of the expert axis. Among the 128 tokens of one device no expert is named more than 2 times, a bound that some block reaches.
All inputs are finite; a program needn't handle non-finite values.
Results may differ from a plain program's by a relative error of at most 0.0058.
Values may be sent and summed in bfloat16 or wider, within the bound.
A program may use at most 128 MiB of HBM per device.

v0:
```python
import jax
import jax.numpy as jnp
from jax import lax
from jax.sharding import PartitionSpec as P

CAP = 2


def contract(left, right, left_dim, right_dim):
    return lax.dot_general(
        left, right, (((left_dim,), (right_dim,)), ((), ())), preferred_element_type=jnp.float32
    )


def block_backward(rows_tok, rows_cot, pair_weights, down_weights):
    pre_gate = jnp.dot(rows_tok, pair_weights[0], preferred_element_type=jnp.float32)
    pre_up = jnp.dot(rows_tok, pair_weights[1], preferred_element_type=jnp.float32)
    sigmoid_gate = jax.nn.sigmoid(pre_gate)
    activated = pre_gate * sigmoid_gate
    hidden = (activated * pre_up).astype(jnp.bfloat16)
    hidden_grad = contract(rows_cot, down_weights, 1, 1)
    gate_grad = (
        hidden_grad * pre_up * sigmoid_gate * (1.0 + pre_gate * (1.0 - sigmoid_gate))
    ).astype(jnp.bfloat16)
    up_grad = (hidden_grad * activated).astype(jnp.bfloat16)
    total_down = contract(hidden, rows_cot, 0, 0)
    total_gate = contract(rows_tok, gate_grad, 0, 0)
    total_up = contract(rows_tok, up_grad, 0, 0)
    input_rows = contract(gate_grad, pair_weights[0], 1, 1) + contract(
        up_grad, pair_weights[1], 1, 1
    )
    return (total_gate, total_up, total_down, input_rows)


def expert_rows(rows_tok, rows_cot, pair_weights, down_weights):
    row_count = rows_tok.shape[0]
    block_rows = min(256, row_count)
    model_width = rows_tok.shape[1]
    unit_count = down_weights.shape[0]
    alive_flag = jnp.any(rows_cot != 0, axis=1).astype(jnp.int32)
    ordering = jnp.argsort(1 - alive_flag, stable=True)
    live_count = jnp.sum(alive_flag)
    block_count = (live_count + block_rows - 1) // block_rows

    def advance(counter, carry_state):
        total_gate, total_up, total_down, input_all = carry_state
        picked = lax.dynamic_slice_in_dim(ordering, counter * block_rows, block_rows)
        part_tok = jnp.take(rows_tok, picked, axis=0)
        part_cot = jnp.take(rows_cot, picked, axis=0)
        more_gate, more_up, more_down, input_rows = block_backward(
            part_tok, part_cot, pair_weights, down_weights
        )
        input_all = input_all.at[picked].set(input_rows)
        return (total_gate + more_gate, total_up + more_up, total_down + more_down, input_all)

    initial = (
        jnp.zeros((model_width, unit_count), jnp.float32),
        jnp.zeros((model_width, unit_count), jnp.float32),
        jnp.zeros((unit_count, model_width), jnp.float32),
        jnp.zeros((row_count, model_width), jnp.float32),
    )
    total_gate, total_up, total_down, input_all = lax.fori_loop(0, block_count, advance, initial)
    return (jnp.stack([total_gate, total_up]), total_down, input_all)


def per_device(activations, cotangent, expert_ids, gate_probs, gate_up, down_proj):
    experts = lax.axis_size("expert")
    identity = expert_ids[:, 0]
    in_window = identity < experts
    onehot = (identity[:, None] == jnp.arange(experts, dtype=jnp.int32)[None, :]).astype(jnp.int32)
    before = jnp.cumsum(onehot, axis=0) - onehot
    ranking = jnp.sum(before * onehot, axis=1)
    slot_index = identity * CAP + ranking
    slot_index = jnp.where(in_window, slot_index, -1)
    placing = (slot_index[None, :] == jnp.arange(experts * CAP, dtype=jnp.int32)[:, None]).astype(
        jnp.bfloat16
    )
    scaled = (gate_probs * cotangent.astype(jnp.float32)).astype(jnp.bfloat16)
    send_tok = jnp.dot(placing, activations, preferred_element_type=jnp.float32).astype(
        jnp.bfloat16
    )
    send_cot = jnp.dot(placing, scaled, preferred_element_type=jnp.float32).astype(jnp.bfloat16)
    got_tok, got_cot = (
        lax.all_to_all(send_tok, "expert", split_axis=0, concat_axis=0, tiled=True),
        lax.all_to_all(send_cot, "expert", split_axis=0, concat_axis=0, tiled=True),
    )
    all_tok, all_cot = (
        lax.all_gather(got_tok, "dp", axis=0, tiled=True),
        lax.all_gather(got_cot, "dp", axis=0, tiled=True),
    )
    own_pair = gate_up[0]
    own_down = down_proj[0]
    pair_total, down_total, partial_value = expert_rows(all_tok, all_cot, own_pair, own_down)
    summed = lax.psum_scatter(partial_value, "dp", scatter_dimension=0, tiled=True)
    rounded = summed.astype(jnp.bfloat16)
    returned = lax.all_to_all(rounded, "expert", split_axis=0, concat_axis=0, tiled=True)
    input_grad = contract(placing, returned, 0, 0).astype(jnp.bfloat16)
    return (
        input_grad,
        pair_total[None].astype(jnp.bfloat16),
        down_total[None].astype(jnp.bfloat16),
    )


def solution(mesh):
    in_specs = (
        P(("dp", "expert"), None),
        P(("dp", "expert"), None),
        P(("dp", "expert"), None),
        P(("dp", "expert"), None),
        P("expert", None, None, "dp"),
        P("expert", "dp", None),
    )
    out_specs = (P(("dp", "expert"), None), P("expert", None, None, "dp"), P("expert", "dp", None))
    return jax.shard_map(
        per_device, mesh=mesh, in_specs=in_specs, out_specs=out_specs, check_vma=False
    )
```

profile of v0, /device:TPU:1, one launch (start us, length us, event | category | flops | bytes accessed | tf_op | source)
XLA Modules:
  0.0 565.2 jit_solution(4953973455181101589)
XLA Ops:
  7.2 0.0 copy-start
  7.2 0.0 all-gather.3.cloned.1.call-start
  7.2 0.8 fusion.18
  8.0 0.2 reduce_window_sum.11
  8.2 0.8 select_reduce_fusion
  9.1 0.7 compare_select_fusion.1
  9.7 1.6 convolution_convert_fusion.2
  11.4 0.3 all_to_all.24
  11.7 26.2 %all_to_all.36 = bf16[32,2,4096]{2,1,0:T(2,128)(2,1)S(1)} all-to-all(bf16[32,2,4096]{2,1,0:T(2,128)(2,1)S(1)} %all_to_all.24), channel_id=1, replica_groups=mesh['dp'=8,'expert'=32] {'expert'}, dimensions={0} | all-to-all | bytes 1048576 | tf_op jit(solution)/shard_map/all_to_all | solution.py:85
  37.9 1.0 all_to_all.26
  38.9 0.0 all-gather.3.cloned.1.call-update
  38.9 0.0 all-gather.5.cloned.1.call-start
  39.0 0.0 copy-done
  39.0 0.3 convolution_convert_fusion.1
  39.3 0.0 copy-done.8
  39.3 0.3 all_to_all.27
  39.7 31.5 %all_to_all.37 = bf16[32,2,4096]{2,1,0:T(2,128)(2,1)S(1)} all-to-all(bf16[32,2,4096]{2,1,0:T(2,128)(2,1)S(1)} %all_to_all.27), channel_id=1, replica_groups=mesh['dp'=8,'expert'=32] {'expert'}, dimensions={0} | all-to-all | bytes 1048576 | tf_op jit(solution)/shard_map/all_to_all | solution.py:84
  71.2 1.0 all_to_all.29
  72.2 0.0 all-gather.5.cloned.1.call-update
  72.2 0.0 reduce-scatter.2.cloned.1.call-start
  72.3 6.1 %copy.9 = bf16[1,2,4096,192]{3,2,1,0:T(8,128)(2,1)} copy(bf16[1,2,4096,192]{2,3,1,0:T(8,128)(2,1)} %param.14) | data formatting | bytes 6291456 | tf_op args[4]
  78.3 68.2 %all-gather.3.cloned.1.call-done = bf16[512,4096]{1,0:T(8,128)(2,1)} async-done(((bf16[64,4096]{1,0:T(8,128)(2,1)}), bf16[512,4096]{1,0:T(8,128)(2,1)}) %all-gather.3.cloned.1.call-update) | async-done | bytes 4194320 | tf_op jit(solution)/shard_map/all_gather | solution.py:89
  146.5 3.3 compare_reduce_fusion
  149.9 0.6 convert_subtract_fusion
  151.2 3.8 sort.17
  154.9 96.6 %all-gather.5.cloned.1.call-done = bf16[512,4096]{1,0:T(8,128)(2,1)} async-done(((bf16[64,4096]{1,0:T(8,128)(2,1)}), bf16[512,4096]{1,0:T(8,128)(2,1)}) %all-gather.5.cloned.1.call-update) | async-done | bytes 4194320 | tf_op jit(solution)/shard_map/all_gather | solution.py:88
  251.5 2.1 broadcast.32.clone
  253.6 2.1 broadcast_in_dim.28
  255.7 2.0 broadcast.32
  257.7 4.2 broadcast_in_dim.29
  262.0 46.4 %while.16 = (s32[]{:T(128)}, f32[4096,192]{0,1:T(8,128)}, f32[4096,192]{0,1:T(8,128)}, f32[192,4096]{1,0:T(8,128)}, f32[512,4096]{1,0:T(8,128)}, /*index=5*/s32[...) while((s32[]{:T(128)}, f32[4096,192]{0,1:T(8,128)}, ...), condition=%wide.region_7.9_spmd, body=%wide.region_5.8_spmd.sunk | while | flops 3231861248 | bytes 160641424 | solution.py:62
  262.0 0.1 compare_and_fusion.2
  262.1 6.6 %gather_fusion = bf16[256,4096]{1,0:T(8,128)(2,1)S(1)} fusion(bf16[512,4096]{1,0:T(8,128)(2,1)} %get-tuple-element.214, s32[1024]{0:T(1024)S(1)} %pad_clamp_fusion.2), kind=kCustom, calls=%fused_computation.clone.clone.1 | custom fusion | bytes 4195328 | tf_op jit(solution)/shard_map/while/body/jit(_take)/gather | solution.py:48
  268.7 0.0 copy-start.6
  268.7 2.8 fusion.51
  271.5 0.0 copy-done.6
  271.5 1.1 fusion.50
  272.6 7.9 %gather_fusion.1 = bf16[256,4096]{1,0:T(8,128)(2,1)} fusion(bf16[512,4096]{1,0:T(8,128)(2,1)} %get-tuple-element.215, s32[1024]{0:T(1024)S(1)} %pad_clamp_fusion.2), kind=kCustom, calls=%fused_computation.1.clone.clone.1 | custom fusion | bytes 4195328 | tf_op jit(solution)/shard_map/while/body/jit(_take)/gather | solution.py:49
  280.6 3.1 multiply_convert_fusion.9
  283.7 0.0 copy-done.1
  283.7 0.0 copy-start.4
  283.7 4.5 convolution_add_fusion.10
  288.2 0.0 copy-done.4
  288.2 0.9 convolution_add_fusion.8
  289.1 0.0 copy-start.5
  289.1 1.7 copy-done.5
  290.8 0.0 copy-done.2
  290.8 0.9 convolution_add_fusion.9
  291.7 1.7 copy-done.3
  293.5 0.3 copy-done.7
  293.8 0.8 fusion.52
  294.6 2.7 convolution_add_fusion.11
  297.3 11.1 %scatter_fusion = f32[512,4096]{1,0:T(8,128)} fusion(f32[512,4096]{1,0:T(8,128)} %get-tuple-element.196, s32[256]{0:T(256)S(1)} %get-tuple-element.173, f32[256,4096]{1,0:T(8,128)} %convolution_add_fusion.11), kind=kCustom, calls=%fused_computation.2.clone.1 | custom fusion | bytes 12583936 | tf_op jit(solution)/shard_map/while/body/scatter | solution.py:53
  308.4 0.0 reduce-scatter.2.cloned.1.call-update
  308.4 4.4 convert_bitcast_fusion.1
  312.9 217.2 %reduce-scatter.2.cloned.1.call-done = f32[64,4096]{1,0:T(8,128)} async-done(((f32[512,4096]{1,0:T(8,128)}), f32[64,4096]{1,0:T(8,128)}) %reduce-scatter.2.cloned.1.call-update) | async-done | bytes 1048592 | tf_op jit(solution)/shard_map/reduce_scatter | solution.py:94
  530.1 1.3 convert_element_type.55
  531.4 1.1 all_to_all.30
  532.5 8.1 %all-to-all-start.2 = ((bf16[32,2,4096]{2,1,0:T(2,128)(2,1)}), bf16[32,2,4096]{2,1,0:T(2,128)(2,1)S(1)}, u32[]{:S(2)}, u32[]{:S(2)}) async-start(bf16[32,2,4096]{2,1,0:T(2,128)(2,1)} %all_to_all.30), calls=%async_computation.3 | async-start | bytes 1048576 | tf_op jit(solution)/shard_map/all_to_all | solution.py:96
  540.6 3.4 pad_maximum_fusion
  544.0 3.2 convert_bitcast_fusion
  547.2 9.8 %all-to-all-done.2 = bf16[32,2,4096]{2,1,0:T(2,128)(2,1)S(1)} async-done(((bf16[32,2,4096]{2,1,0:T(2,128)(2,1)}), bf16[32,2,4096]{2,1,0:T(2,128)(2,1)S(1)}, u32[]{:S(2)}, u32[]{:S(2)}) %all-to-all-start.2) | async-done | bytes 524320 | tf_op jit(solution)/shard_map/all_to_all | solution.py:96
  557.1 0.2 all_to_all.32
  557.3 1.5 convolution_convert_fusion
  (9 shorter events, 0.0 us)
Async XLA Ops:
  7.2 31.8 %copy-start = (bf16[128,4096]{1,0:T(8,128)(2,1)S(1)}, bf16[128,4096]{1,0:T(8,128)(2,1)}, u32[]{:S(2)}) copy-start(bf16[128,4096]{1,0:T(8,128)(2,1)} %param.10) | copy-start | bytes 3145732
  7.2 139.4 %all-gather.3.cloned.1.call-start = ((), (), s32[]{:S(2)}) async-start(), calls=%async_computation.4 | async-start | bytes 4718592 | tf_op jit(solution)/shard_map/all_gather | solution.py:89
  9.7 29.6 %copy-start.8 = (s32[128]{0:T(128)}, s32[128]{0:T(128)S(1)}, u32[]{:S(2)}) copy-start(s32[128]{0:T(128)S(1)} %compare_select_fusion.1) | copy-start | bytes 1540
  38.9 212.6 %all-gather.5.cloned.1.call-start = ((), (), s32[]{:S(2)}) async-start(), calls=%async_computation.5 | async-start | bytes 4718592 | tf_op jit(solution)/shard_map/all_gather | solution.py:88
  72.2 457.9 %reduce-scatter.2.cloned.1.call-start = ((), (), s32[]{:S(2)}) async-start(), calls=%async_computation.6 | async-start | bytes 9437184 | tf_op jit(solution)/shard_map/reduce_scatter | solution.py:94
  268.7 2.8 copy-start.6
  280.6 3.1 copy-start.1
  283.7 4.5 copy-start.4
  288.2 2.6 copy-start.2
  289.1 1.7 copy-start.5
  290.8 3.0 copy-start.7
  291.7 1.8 copy-start.3
  532.5 24.6 %all-to-all-start.2 = ((bf16[32,2,4096]{2,1,0:T(2,128)(2,1)}), bf16[32,2,4096]{2,1,0:T(2,128)(2,1)S(1)}, u32[]{:S(2)}, u32[]{:S(2)}) async-start(bf16[32,2,4096]{2,1,0:T(2,128)(2,1)} %all_to_all.30), calls=%async_computation.3 | async-start | bytes 1048576 | tf_op jit(solution)/shard_map/all_to_all | solution.py:96
  544.0 13.3 %copy-start.9 = (s32[128]{0:T(128)S(1)}, s32[128]{0:T(128)}, u32[]{:S(2)}) copy-start(s32[128]{0:T(128)} %copy-done.8) | copy-start | bytes 1540
Sparse Core Ops, SparseCore 0:
  39.1 107.4 all-gather.2
  149.7 101.7 all-gather.4
  308.5 221.5 reduce-scatter.1
where the time goes:
time: 566 us; the launch traced here: 565 us
  waiting for transfers between devices  392 us (69%)
  blocking collectives  57.8 us (10%)
  local copies, waits for them, and re-layouts  49.9 us (9%)
  other arithmetic  22.6 us (4%)
  matrix products  20.2 us (4%)
  between operations  14.5 us (3%)
  starting transfers between devices  8.24 us (1%)
    reduce_scatter x1, waiting for transfers between devices, per_device(): lax.psum_scatter(partial_value, 'dp', scatter_dimension=0, tiled=True)  217 us
    all_gather x1, waiting for transfers between devices, per_device(): lax.all_gather(got_tok, 'dp', axis=0, tiled=True)  96.6 us
    all_gather x1, waiting for transfers between devices, per_device(): lax.all_gather(got_cot, 'dp', axis=0, tiled=True)  68.2 us
    all_to_all x1, blocking collectives, per_device(): lax.all_to_all(send_tok, 'expert', split_axis=0, concat_axis=0, tiled=True)  31.5 us
    all_to_all x1, blocking collectives, per_device(): lax.all_to_all(send_cot, 'expert', split_axis=0, concat_axis=0, tiled=True)  26.2 us
    dot_general x7, matrix products, contract(): lax.dot_general(left, right, (((left_dim,), (right_dim,)), ((), ())), pre...  14.4 us
  transfers between devices with their start and end apart: 4, of which 4 were waited for; matrix products, arithmetic and copies ran while one was open for 4% of the time, Pallas kernels for 0%

commit v1 on v0

--- a/solution.py
+++ b/solution.py
@@ -85,7 +85,9 @@
         lax.all_to_all(send_cot, "expert", split_axis=0, concat_axis=0, tiled=True),
     )
     all_tok, all_cot = (
-        lax.all_gather(got_tok, "dp", axis=0, tiled=True),
+        jnp.concatenate(
+            lax.all_to_all(jnp.stack([got_tok] * lax.axis_size("dp")), "dp", 0, 0), axis=0
+        ),
         lax.all_gather(got_cot, "dp", axis=0, tiled=True),
     )
     own_pair = gate_up[0]

time: 566 us -> 545 us (0.963)
  blocking collectives: 57.8 us -> 0 us
  starting transfers between devices: 8.24 us -> 30.4 us
  waiting for transfers between devices: 392 us -> 402 us
    all_gather x1 -> x0, waiting for transfers between devices: 96.6 us -> none  [per_device(): lax.all_gather(got_tok, 'dp', axis=0, tiled=True)]
    all_gather x1, waiting for transfers between devices: 68.2 us -> 148 us  [per_device(): lax.all_gather(got_cot, 'dp', axis=0, tiled=True)]
    all_to_all x2 -> x0, blocking collectives: 57.8 us -> none  [the longest x1 31.5 us: per_device(): lax.all_to_all(send_tok, 'expert', split_axis=0, concat_axis=0, tiled=True)]
    all_to_all x0 -> x3, waiting for transfers between devices: none -> 30.3 us  [the longest x1 15.4 us: per_device(): lax.all_to_all(send_tok, 'expert', split_axis=0, concat_axis=0, tiled=True)]
    all_to_all x0 -> x3, starting transfers between devices: none -> 22.2 us  [the longest x1 10 us: per_device(): lax.all_to_all(send_cot, 'expert', split_axis=0, concat_axis=0, tiled=True)]
  transfers between devices with their start and end apart: 4 -> 6, of which waited for: 4 -> 5; matrix products, arithmetic and copies ran while one was open for 4% -> 5% of each run, Pallas kernels for 0% -> 0%
where the time goes in v1:
time: 545 us; the launch traced here: 544 us
  waiting for transfers between devices  402 us (74%)
  local copies, waits for them, and re-layouts  53.1 us (10%)
  starting transfers between devices  30.4 us (6%)
  other arithmetic  22.7 us (4%)
  matrix products  20.3 us (4%)
  between operations  14.8 us (3%)
    reduce_scatter x1, waiting for transfers between devices, per_device(): lax.psum_scatter(partial_value, 'dp', scatter_dimension=0, tiled=True)  214 us
    all_gather x1, waiting for transfers between devices, per_device(): lax.all_gather(got_cot, 'dp', axis=0, tiled=True)  148 us
    all_to_all x1, waiting for transfers between devices, per_device(): lax.all_to_all(send_tok, 'expert', split_axis=0, concat_axis=0, tiled=True)  15.4 us
    all_to_all x1, waiting for transfers between devices, per_device(): lax.all_to_all(send_cot, 'expert', split_axis=0, concat_axis=0, tiled=True)  15 us
    dot_general x7, matrix products, contract(): lax.dot_general(left, right, (((left_dim,), (right_dim,)), ((), ())), pre...  14.4 us
    scatter x1, local copies, waits for them, and re-layouts, advance(): input_all = input_all.at[picked].set(input_rows)  11.1 us
  transfers between devices with their start and end apart: 6, of which 5 were waited for; matrix products, arithmetic and copies ran while one was open for 5% of the time, Pallas kernels for 0%

profile of v1, /device:TPU:1, one launch (start us, length us, event | category | flops | bytes accessed | tf_op | source)
XLA Modules:
  0.0 543.5 jit_solution(11456009413045295143)
XLA Ops:
  7.2 0.0 copy-start
  7.2 0.8 fusion.18
  8.0 0.2 reduce_window_sum.11
  8.2 0.8 select_reduce_fusion
  9.0 0.7 compare_select_fusion.1
  9.7 1.6 convolution_convert_fusion.2
  11.3 1.1 all_to_all.25
  12.5 10.0 %all-to-all-start = ((bf16[32,2,4096]{2,1,0:T(2,128)(2,1)}), bf16[32,2,4096]{2,1,0:T(2,128)(2,1)S(1)}, u32[]{:S(2)}, u32[]{:S(2)}) async-start(bf16[32,2,4096]{2,1,0:T(2,128)(2,1)} %all_to_all.25), calls=%async_computation | async-start | bytes 1048576 | tf_op jit(solution)/shard_map/all_to_all | solution.py:85
  22.5 0.0 copy-done
  22.5 0.3 convolution_convert_fusion.1
  22.8 1.1 all_to_all.28
  23.9 0.0 copy-done.9
  23.9 15.0 %all-to-all-done = bf16[32,2,4096]{2,1,0:T(2,128)(2,1)S(1)} async-done(((bf16[32,2,4096]{2,1,0:T(2,128)(2,1)}), bf16[32,2,4096]{2,1,0:T(2,128)(2,1)S(1)}, u32[]{:S(2)}, u32[]{:S(2)}) %all-to-all-start) | async-done | bytes 524320 | tf_op jit(solution)/shard_map/all_to_all | solution.py:85
  38.9 4.1 all-to-all-start.1
  43.0 0.0 all-gather.2.cloned.1.call-start
  43.0 1.0 all_to_all.27
  44.0 0.0 all-gather.2.cloned.1.call-update
  44.1 15.4 %all-to-all-done.1 = bf16[32,2,4096]{2,1,0:T(2,128)(2,1)S(1)} async-done(((bf16[32,2,4096]{2,1,0:T(2,128)(2,1)}), bf16[32,2,4096]{2,1,0:T(2,128)(2,1)S(1)}, u32[]{:S(2)}, u32[]{:S(2)}) %all-to-all-start.1) | async-done | bytes 524320 | tf_op jit(solution)/shard_map/all_to_all | solution.py:84
  59.4 0.2 stack.10
  59.6 2.5 stack.11
  62.1 8.1 %all-to-all-start.2 = ((bf16[8,64,4096]{2,1,0:T(8,128)(2,1)}), bf16[8,64,4096]{2,1,0:T(8,128)(2,1)}, u32[]{:S(2)}, u32[]{:S(2)}) async-start(bf16[8,64,4096]{2,1,0:T(8,128)(2,1)} %stack.11), calls=%async_computation.2 | async-start | bytes 8388608 | tf_op jit(solution)/shard_map/all_to_all | solution.py:89
  70.2 0.0 reduce-scatter.2.cloned.1.call-start
  70.3 6.0 %copy.9 = bf16[1,2,4096,192]{3,2,1,0:T(8,128)(2,1)} copy(bf16[1,2,4096,192]{2,3,1,0:T(8,128)(2,1)} %param.14) | data formatting | bytes 6291456 | tf_op args[4]
  76.3 147.6 %all-gather.2.cloned.1.call-done = bf16[512,4096]{1,0:T(8,128)(2,1)} async-done(((bf16[64,4096]{1,0:T(8,128)(2,1)}), bf16[512,4096]{1,0:T(8,128)(2,1)}) %all-gather.2.cloned.1.call-update) | async-done | bytes 4194320 | tf_op jit(solution)/shard_map/all_gather | solution.py:91
  223.9 3.3 compare_reduce_fusion
  227.2 0.6 convert_subtract_fusion
  228.5 3.8 sort.17
  232.3 0.0 all-to-all-done.2
  232.3 2.1 broadcast.33.clone
  234.4 2.1 broadcast_in_dim.28
  236.5 2.0 broadcast.33
  238.5 4.3 broadcast_in_dim.29
  242.8 46.4 %while.16 = (s32[]{:T(128)}, f32[4096,192]{0,1:T(8,128)}, f32[4096,192]{0,1:T(8,128)}, f32[192,4096]{1,0:T(8,128)}, f32[512,4096]{1,0:T(8,128)}, /*index=5*/s32[...) while((s32[]{:T(128)}, f32[4096,192]{0,1:T(8,128)}, ...), condition=%wide.region_7.9_spmd, body=%wide.region_5.8_spmd.sunk | while | flops 3231861248 | bytes 160641424 | solution.py:62
  242.8 0.1 compare_and_fusion.2
  242.8 6.6 %gather_fusion = bf16[256,4096]{1,0:T(8,128)(2,1)S(1)} fusion(bf16[512,4096]{1,0:T(8,128)(2,1)} %get-tuple-element.214, s32[1024]{0:T(1024)S(1)} %pad_clamp_fusion.2), kind=kCustom, calls=%fused_computation.clone.clone.1 | custom fusion | bytes 4195328 | tf_op jit(solution)/shard_map/while/body/jit(_take)/gather | solution.py:48
  249.5 2.8 fusion.51
  252.3 0.0 copy-done.7
  252.3 1.1 fusion.50
  253.4 7.9 %gather_fusion.1 = bf16[256,4096]{1,0:T(8,128)(2,1)} fusion(bf16[512,4096]{1,0:T(8,128)(2,1)} %get-tuple-element.215, s32[1024]{0:T(1024)S(1)} %pad_clamp_fusion.2), kind=kCustom, calls=%fused_computation.1.clone.clone.1 | custom fusion | bytes 4195328 | tf_op jit(solution)/shard_map/while/body/jit(_take)/gather | solution.py:49
  261.3 3.1 multiply_convert_fusion.9
  264.5 0.0 copy-start.5
  264.5 4.5 convolution_add_fusion.10
  269.0 0.9 convolution_add_fusion.8
  269.9 0.0 copy-start.6
  269.9 1.7 copy-done.6
  271.6 0.0 copy-done.3
  271.6 0.9 convolution_add_fusion.9
  272.5 1.7 copy-done.4
  274.2 0.3 copy-done.8
  274.5 0.8 fusion.52
  275.3 2.8 convolution_add_fusion.11
  278.1 11.1 %scatter_fusion = f32[512,4096]{1,0:T(8,128)} fusion(f32[512,4096]{1,0:T(8,128)} %get-tuple-element.196, s32[256]{0:T(256)S(1)} %get-tuple-element.173, f32[256,4096]{1,0:T(8,128)} %convolution_add_fusion.11), kind=kCustom, calls=%fused_computation.2.clone.1 | custom fusion | bytes 12583936 | tf_op jit(solution)/shard_map/while/body/scatter | solution.py:53
  289.2 0.0 reduce-scatter.2.cloned.1.call-update
  289.2 4.4 convert_bitcast_fusion.1
  293.7 214.4 %reduce-scatter.2.cloned.1.call-done = f32[64,4096]{1,0:T(8,128)} async-done(((f32[512,4096]{1,0:T(8,128)}), f32[64,4096]{1,0:T(8,128)}) %reduce-scatter.2.cloned.1.call-update) | async-done | bytes 1048592 | tf_op jit(solution)/shard_map/reduce_scatter | solution.py:96
  508.0 1.3 convert_element_type.55
  509.3 1.1 all_to_all.31
  510.5 8.1 %all-to-all-start.3 = ((bf16[32,2,4096]{2,1,0:T(2,128)(2,1)}), bf16[32,2,4096]{2,1,0:T(2,128)(2,1)S(1)}, u32[]{:S(2)}, u32[]{:S(2)}) async-start(bf16[32,2,4096]{2,1,0:T(2,128)(2,1)} %all_to_all.31), calls=%async_computation.4 | async-start | bytes 1048576 | tf_op jit(solution)/shard_map/all_to_all | solution.py:98
  518.6 3.4 pad_maximum_fusion
  522.0 3.3 convert_bitcast_fusion
  525.3 9.7 %all-to-all-done.3 = bf16[32,2,4096]{2,1,0:T(2,128)(2,1)S(1)} async-done(((bf16[32,2,4096]{2,1,0:T(2,128)(2,1)}), bf16[32,2,4096]{2,1,0:T(2,128)(2,1)S(1)}, u32[]{:S(2)}, u32[]{:S(2)}) %all-to-all-start.3) | async-done | bytes 524320 | tf_op jit(solution)/shard_map/all_to_all | solution.py:98
  535.0 0.2 all_to_all.33
  535.2 0.0 copy-done.10
  535.2 1.5 convolution_convert_fusion
  (13 shorter events, 0.0 us)
Async XLA Ops:
  7.2 15.3 %copy-start = (bf16[128,4096]{1,0:T(8,128)(2,1)S(1)}, bf16[128,4096]{1,0:T(8,128)(2,1)}, u32[]{:S(2)}) copy-start(bf16[128,4096]{1,0:T(8,128)(2,1)} %param.10) | copy-start | bytes 3145732
  9.7 14.2 %copy-start.9 = (s32[128]{0:T(128)}, s32[128]{0:T(128)S(1)}, u32[]{:S(2)}) copy-start(s32[128]{0:T(128)S(1)} %compare_select_fusion.1) | copy-start | bytes 1540
  12.5 26.4 %all-to-all-start = ((bf16[32,2,4096]{2,1,0:T(2,128)(2,1)}), bf16[32,2,4096]{2,1,0:T(2,128)(2,1)S(1)}, u32[]{:S(2)}, u32[]{:S(2)}) async-start(bf16[32,2,4096]{2,1,0:T(2,128)(2,1)} %all_to_all.25), calls=%async_computation | async-start | bytes 1048576 | tf_op jit(solution)/shard_map/all_to_all | solution.py:85
  38.9 20.5 %all-to-all-start.1 = ((bf16[32,2,4096]{2,1,0:T(2,128)(2,1)}), bf16[32,2,4096]{2,1,0:T(2,128)(2,1)S(1)}, u32[]{:S(2)}, u32[]{:S(2)}) async-start(bf16[32,2,4096]{2,1,0:T(2,128)(2,1)} %all_to_all.28), calls=%async_computation.1 | async-start | bytes 1048576 | tf_op jit(solution)/shard_map/all_to_all | solution.py:84
  43.0 180.9 %all-gather.2.cloned.1.call-start = ((), (), s32[]{:S(2)}) async-start(), calls=%async_computation.5 | async-start | bytes 4718592 | tf_op jit(solution)/shard_map/all_gather | solution.py:91
  62.1 170.2 %all-to-all-start.2 = ((bf16[8,64,4096]{2,1,0:T(8,128)(2,1)}), bf16[8,64,4096]{2,1,0:T(8,128)(2,1)}, u32[]{:S(2)}, u32[]{:S(2)}) async-start(bf16[8,64,4096]{2,1,0:T(8,128)(2,1)} %stack.11), calls=%async_computation.2 | async-start | bytes 8388608 | tf_op jit(solution)/shard_map/all_to_all | solution.py:89
  70.2 437.8 %reduce-scatter.2.cloned.1.call-start = ((), (), s32[]{:S(2)}) async-start(), calls=%async_computation.6 | async-start | bytes 9437184 | tf_op jit(solution)/shard_map/reduce_scatter | solution.py:96
  249.5 2.8 copy-start.7
  261.3 3.1 copy-start.2
  264.5 4.5 copy-start.5
  269.0 2.6 copy-start.3
  269.9 1.7 copy-start.6
  271.6 3.0 copy-start.8
  272.5 1.7 copy-start.4
  510.5 24.6 %all-to-all-start.3 = ((bf16[32,2,4096]{2,1,0:T(2,128)(2,1)}), bf16[32,2,4096]{2,1,0:T(2,128)(2,1)S(1)}, u32[]{:S(2)}, u32[]{:S(2)}) async-start(bf16[32,2,4096]{2,1,0:T(2,128)(2,1)} %all_to_all.31), calls=%async_computation.4 | async-start | bytes 1048576 | tf_op jit(solution)/shard_map/all_to_all | solution.py:98
  521.9 13.3 %copy-start.10 = (s32[128]{0:T(128)S(1)}, s32[128]{0:T(128)}, u32[]{:S(2)}) copy-start(s32[128]{0:T(128)} %copy-done.9) | copy-start | bytes 1540
  522.0 14.7 %copy-start.1 = (bf16[128,4096]{1,0:T(8,128)(2,1)S(1)}, bf16[128,4096]{1,0:T(8,128)(2,1)}, u32[]{:S(2)}) copy-start(bf16[128,4096]{1,0:T(8,128)(2,1)} %param.10) | copy-start | bytes 3145732
Sparse Core Ops, SparseCore 0:
  47.0 176.8 all-gather.1
  289.3 218.6 reduce-scatter.1
